TPU v7x, 512 devices: a whole 4x4x16 slice. The times are simulated.
512 devices in a mesh: expert: 64 (over x, z), dp: 4 (over y), test: 2 (over core).
Axes of the slice: x: 4, y: 4, z: 16, core: 2. Of those that a mesh axis runs over, the one named last changes fastest.
Arguments:
- tokens: bfloat16 [16384, 3584], P(('expert', 'dp'), 'test'), may hold values from -6 to 6
- out_grad: bfloat16 [16384, 3584], P(('expert', 'dp'), 'test'), may hold values from -6 to 6
- route_ids: int32 [16384, 8], P(('expert', 'dp')), may hold values from 0 to 255, as said below
- route_slots: int32 [16384, 8], P(('expert', 'dp')), may hold values from -1 to 1, as said below
- route_weight: bfloat16 [16384, 8], P(('expert', 'dp')), may hold values from 0.19921875 to 1
- w_gate: bfloat16 [64, 3584, 1024], P('expert', None, ('dp', 'test')), may hold values from -0.09375 to 0.09375
- w_up: bfloat16 [64, 3584, 1024], P('expert', None, ('dp', 'test')), may hold values from -0.09375 to 0.09375
- w_down: bfloat16 [64, 1024, 3584], P('expert', ('dp', 'test')), may hold values from -0.1875 to 0.1875
- proj_hidden: bfloat16 [64, 64, 1024], P('expert', None, ('dp', 'test')), may hold values from -0.1875 to 0.1875
- proj_grad: bfloat16 [64, 64, 3584], P('expert'), may hold values from -0.09375 to 0.09375
- test_feats: bfloat16 [64, 256, 4096], P('expert', 'test'), may hold values from -0.09375 to 0.09375
Outputs:
- in_grad: bfloat16 [16384, 3584], P(('expert', 'dp'), 'test')
- scores: float32 [16384, 256], P(('expert', 'dp'), 'test')
Inputs may be any that keep to these rules, and one draw needn't show every extreme that they name: `route_ids`: each row names 8 different experts. `route_slots`: A route's slot is -1 exactly when its expert is 64 or more, or when 2 earlier tokens of the same aligned block of 64 rows already take that expert; otherwise it is the number of earlier tokens of that block routed to that expert.
All inputs are finite; a program needn't handle non-finite values.
Results may differ from a plain program's by a relative error of at most 0.0065.
Values may be sent and summed in bfloat16 or wider, within the bound.
A program may use at most 64 MiB of HBM per device.

v0:
```python
import jax
import jax.numpy as jnp
from jax import lax
from jax.sharding import PartitionSpec as P

CAP = 2


def pick_tables(ids_in, slots_in, weights_in, experts):
    live_mask = (slots_in >= 0) & (ids_in < experts)
    slot_code = jnp.where(live_mask, ids_in * CAP + slots_in, -1)
    columns = jnp.arange(experts * CAP, dtype=jnp.int32)
    matches = slot_code[:, :, None] == columns[None, None, :]
    picks = jnp.sum(matches.astype(jnp.float32), axis=1)
    weighted = jnp.sum(jnp.where(matches, weights_in.astype(jnp.float32)[:, :, None], 0.0), axis=1)
    return (picks.astype(jnp.bfloat16), weighted.astype(jnp.bfloat16))


def dot(a, b, ca, cb):
    return lax.dot_general(a, b, (((ca,), (cb,)), ((), ())), preferred_element_type=jnp.float32)


def on_device(
    tokens,
    out_grad,
    route_ids,
    route_slots,
    route_weight,
    w_gate,
    w_up,
    w_down,
    proj_hidden,
    proj_grad,
    test_feats,
):
    experts = lax.axis_size("expert")
    groups = lax.axis_size("dp")
    halves = lax.axis_size("test")
    half = tokens.shape[1]
    slots = experts * CAP
    pick, weighted = pick_tables(route_ids, route_slots, route_weight, experts)
    in_buf = dot(pick, tokens, 0, 0).astype(jnp.bfloat16)
    grad_buf = dot(weighted, out_grad, 0, 0).astype(jnp.bfloat16)

    def exchange(rows):
        width = rows.shape[1]
        moved = lax.all_to_all(
            rows.reshape(experts, CAP, width), "expert", split_axis=0, concat_axis=0, tiled=True
        )
        return moved.reshape(slots, width)

    def spread(rows):
        full = lax.all_gather(rows, ("dp", "test"), axis=0, tiled=True)
        full = full.reshape(groups, halves, slots, half)
        return [full[:, h].reshape(groups * slots, half) for h in range(halves)]

    mine_in = exchange(in_buf)
    ins = spread(mine_in)
    mine_grad = exchange(grad_buf)
    grads = spread(mine_grad)
    gate_w, up_w, down_w = (w_gate[0], w_up[0], w_down[0])

    def cut(arr, h, axis):
        return lax.slice_in_dim(arr, h * half, (h + 1) * half, axis=axis)

    gate_pre = sum((dot(ins[h], cut(gate_w, h, 0), 1, 0) for h in range(halves)))
    up_pre = sum((dot(ins[h], cut(up_w, h, 0), 1, 0) for h in range(halves)))
    sig = jax.nn.sigmoid(gate_pre)
    act = gate_pre * sig
    hidden = (act * up_pre).astype(jnp.bfloat16)
    proj_part = dot(hidden, proj_hidden[0], 1, 1)
    hid_grad = sum((dot(grads[h], cut(down_w, h, 1), 1, 1) for h in range(halves)))
    up_grad = (hid_grad * act).astype(jnp.bfloat16)
    gate_grad = (hid_grad * up_pre * sig * (1.0 + gate_pre * (1.0 - sig))).astype(jnp.bfloat16)
    parts = [
        (dot(gate_grad, cut(gate_w, h, 0), 1, 1) + dot(up_grad, cut(up_w, h, 0), 1, 1)).astype(
            jnp.bfloat16
        )
        for h in range(halves)
    ]
    parts = jnp.stack([p.reshape(groups, slots, half) for p in parts], axis=1)
    mine_back = lax.psum_scatter(
        parts.reshape(groups * halves * slots, half),
        ("dp", "test"),
        scatter_dimension=0,
        tiled=True,
    )
    back = exchange(mine_back.astype(jnp.bfloat16))
    in_grad = dot(pick, back, 1, 0).astype(jnp.bfloat16)
    hidden_vec = lax.psum(proj_part, ("dp", "test"))
    me = lax.axis_index("dp")
    hid_mine = lax.dynamic_slice_in_dim(hidden_vec, me * slots, slots, 0)
    grad_mine = sum(
        (
            dot(
                lax.dynamic_slice_in_dim(grads[h], me * slots, slots, 0),
                cut(proj_grad[0], h, 1),
                1,
                1,
            )
            for h in range(halves)
        )
    )
    feature = (hid_mine[:, :, None] * grad_mine[:, None, :]).reshape(slots, -1).astype(jnp.bfloat16)
    score = dot(feature, test_feats[0], 1, 1).astype(jnp.bfloat16)
    scores = dot(pick, exchange(score), 1, 0)
    return (in_grad, scores)


def solution(mesh):
    placed = (
        P(("expert", "dp"), "test"),
        P(("expert", "dp"), "test"),
        P(("expert", "dp"), None),
        P(("expert", "dp"), None),
        P(("expert", "dp"), None),
        P("expert", None, ("dp", "test")),
        P("expert", None, ("dp", "test")),
        P("expert", ("dp", "test"), None),
        P("expert", None, ("dp", "test")),
        P("expert", None, None),
        P("expert", "test", None),
    )
    return jax.shard_map(
        on_device,
        mesh=mesh,
        in_specs=placed,
        out_specs=(P(("expert", "dp"), "test"), P(("expert", "dp"), "test")),
        check_vma=False,
    )
```

profile of v0, /device:TPU:31, one launch (start us, length us, event | category | flops | bytes accessed | tf_op | source)
XLA Modules:
  0.0 316.4 jit_solution(14806735404021677156)
XLA Ops:
  7.2 0.8 add_select_fusion
  8.1 0.8 copy.22
  9.1 1.3 convolution_convert_fusion.1
  10.6 45.3 %all_to_all.20 = bf16[64,2,1792]{2,1,0:T(2,128)(2,1)S(1)} all-to-all(bf16[64,2,1792]{2,1,0:T(2,128)(2,1)S(1)} %reshape.58), channel_id=1, replica_groups=mesh['expert'=64,'dp'=4,'test'=2] {'expert'}, dimensions={0} | all-to-all | bytes 917504 | tf_op jit(solution)/shard_map/all_to_all | solution.py:47
  55.9 1.0 reshape.59
  57.4 34.0 %all_to_all.21 = bf16[64,2,1792]{2,1,0:T(2,128)(2,1)S(1)} all-to-all(bf16[64,2,1792]{2,1,0:T(2,128)(2,1)S(1)} %reshape.61), channel_id=1, replica_groups=mesh['expert'=64,'dp'=4,'test'=2] {'expert'}, dimensions={0} | all-to-all | bytes 917504 | tf_op jit(solution)/shard_map/all_to_all | solution.py:47
  91.4 0.9 reshape.62
  92.4 3.6 %fusion.41 = (bf16[4,1,128,1792]{3,2,1,0:T(8,128)(2,1)}, bf16[4,1,128,1792]{3,2,1,0:T(8,128)(2,1)S(1)}) fusion(bf16[4,2,128,1792]{3,2,1,0:T(8,128)(2,1)} %bitcast.73), kind=kLoop, calls=%fused_computation.61 | loop fusion | bytes 7340032 | tf_op jit(solution)/shard_map/slice | solution.py:55
  96.0 31.3 %all-gather.5.cloned.1.call-done = bf16[1024,1792]{1,0:T(8,128)(2,1)} async-done(((bf16[128,1792]{1,0:T(8,128)(2,1)}), bf16[1024,1792]{1,0:T(8,128)(2,1)}) %all-gather.5.cloned.1.call-update) | async-done | bytes 3670032 | tf_op jit(solution)/shard_map/all_gather | solution.py:53
  127.4 2.4 fusion.42
  129.8 0.6 fusion.9
  131.6 0.6 convolution_add_fusion.1
  132.3 0.6 convolution_add_fusion
  134.5 0.6 multiply_convert_fusion.2
  135.1 2.4 fusion.4
  137.6 2.5 fusion.7
  140.1 0.9 fusion.30
  141.0 3.0 add_convert_fusion
  144.5 0.6 add_convert_fusion.1
  145.2 2.1 pad_maximum_fusion
  147.3 1.0 copy-done.6
  148.6 1.3 convolution_add_fusion.3
  149.9 66.4 %all-reduce.2.cloned.1.call-done = f32[512,64]{0,1:T(8,128)} async-done(((f32[512,64]{0,1:T(8,128)}), f32[512,64]{0,1:T(8,128)}) %all-reduce.2.cloned.1.call-update) | async-done | bytes 131088 | tf_op jit(solution)/shard_map/psum | solution.py:90
  216.3 0.8 constant_dynamic-slice_fusion
  217.4 1.1 convolution_convert_fusion.3
  218.5 15.3 %all-to-all-start.3 = ((bf16[64,2,128]{2,1,0:T(2,128)(2,1)}), bf16[64,2,128]{2,1,0:T(2,128)(2,1)S(1)}, u32[]{:S(2)}, u32[]{:S(2)}) async-start(bf16[64,2,128]{2,1,0:T(2,128)(2,1)} %bitcast.20), calls=%async_computation.4 | async-start | bytes 65536 | tf_op jit(solution)/shard_map/all_to_all | solution.py:47
  233.8 29.1 %reduce-scatter.2.cloned.1.call-done = bf16[128,1792]{1,0:T(8,128)(2,1)} async-done(((bf16[1024,1792]{1,0:T(8,128)(2,1)}), bf16[128,1792]{1,0:T(8,128)(2,1)}) %reduce-scatter.2.cloned.1.call-update) | async-done | bytes 458768 | tf_op jit(solution)/shard_map/reduce_scatter | solution.py:82
  262.9 2.0 reshape.65
  264.9 15.0 %all-to-all-start.2 = ((bf16[64,2,1792]{2,1,0:T(2,128)(2,1)}), bf16[64,2,1792]{2,1,0:T(2,128)(2,1)S(1)}, u32[]{:S(2)}, u32[]{:S(2)}) async-start(bf16[64,2,1792]{2,1,0:T(2,128)(2,1)} %reshape.65), calls=%async_computation.3 | async-start | bytes 917504 | tf_op jit(solution)/shard_map/all_to_all | solution.py:47
  279.9 0.7 fusion.43
  280.6 28.2 %all-to-all-done.2 = bf16[64,2,1792]{2,1,0:T(2,128)(2,1)S(1)} async-done(((bf16[64,2,1792]{2,1,0:T(2,128)(2,1)}), bf16[64,2,1792]{2,1,0:T(2,128)(2,1)S(1)}, u32[]{:S(2)}, u32[]{:S(2)}) %all-to-all-start.2) | async-done | bytes 458784 | tf_op jit(solution)/shard_map/all_to_all | solution.py:47
  309.0 0.9 convolution_convert_fusion.2
  (39 shorter events, 5.2 us)
Async XLA Ops:
  7.2 210.2 %copy-start = (bf16[1,128,4096]{2,1,0:T(8,128)(2,1)S(1)}, bf16[1,128,4096]{2,1,0:T(8,128)(2,1)}, u32[]{:S(2)}) copy-start(bf16[1,128,4096]{2,1,0:T(8,128)(2,1)} %param.21) | copy-start | bytes 3145732
  7.2 85.2 %all-gather.3.cloned.1.call-start = ((), (), s32[]{:S(2)}) async-start(), calls=%async_computation.5 | async-start | bytes 4128768 | tf_op jit(solution)/shard_map/all_gather | solution.py:53
  9.1 47.8 %copy-start.8 = (bf16[64,1792]{1,0:T(8,128)(2,1)S(1)}, bf16[64,1792]{1,0:T(8,128)(2,1)}, u32[]{:S(2)}) copy-start(bf16[64,1792]{1,0:T(8,128)(2,1)} %param.11) | copy-start | bytes 688132
  56.9 70.5 %all-gather.5.cloned.1.call-start = ((), (), s32[]{:S(2)}) async-start(), calls=%async_computation.6 | async-start | bytes 4128768 | tf_op jit(solution)/shard_map/all_gather | solution.py:53
  92.4 124.0 %all-reduce.2.cloned.1.call-start = ((), (), s32[]{:S(2)}) async-start(), calls=%async_computation.8 | async-start | bytes 262144 | tf_op jit(solution)/shard_map/psum | solution.py:90
  127.4 2.4 copy-start.2
  129.8 1.2 copy-start.3
  132.2 1.2 copy-start.7
  132.9 1.6 copy-start.5
  137.6 2.5 copy-start.9
  140.9 122.0 %reduce-scatter.2.cloned.1.call-start = ((), (), s32[]{:S(2)}) async-start(), calls=%async_computation.7 | async-start | bytes 4128768 | tf_op jit(solution)/shard_map/reduce_scatter | solution.py:82
  141.0 3.3 %copy-start.1 = (f32[512,1792]{1,0:T(8,128)S(1)}, f32[512,1792]{1,0:T(8,128)}, u32[]{:S(2)}) copy-start(f32[512,1792]{1,0:T(8,128)} %fusion.7) | copy-start | bytes 11010052
  141.0 3.5 %copy-start.4 = (bf16[1,3584,128]{2,1,0:T(8,128)(2,1)S(1)}, bf16[1,3584,128]{2,1,0:T(8,128)(2,1)}, u32[]{:S(2)}) copy-start(bf16[1,3584,128]{2,1,0:T(8,128)(2,1)} %param.17) | copy-start | bytes 2752516
  147.3 1.0 copy-start.6
  218.5 46.4 %all-to-all-start.3 = ((bf16[64,2,128]{2,1,0:T(2,128)(2,1)}), bf16[64,2,128]{2,1,0:T(2,128)(2,1)S(1)}, u32[]{:S(2)}, u32[]{:S(2)}) async-start(bf16[64,2,128]{2,1,0:T(2,128)(2,1)} %bitcast.20), calls=%async_computation.4 | async-start | bytes 65536 | tf_op jit(solution)/shard_map/all_to_all | solution.py:47
  264.9 43.9 %all-to-all-start.2 = ((bf16[64,2,1792]{2,1,0:T(2,128)(2,1)}), bf16[64,2,1792]{2,1,0:T(2,128)(2,1)S(1)}, u32[]{:S(2)}, u32[]{:S(2)}) async-start(bf16[64,2,1792]{2,1,0:T(2,128)(2,1)} %reshape.65), calls=%async_computation.3 | async-start | bytes 917504 | tf_op jit(solution)/shard_map/all_to_all | solution.py:47
Sparse Core Ops, SparseCore 0:
  57.0 30.6 all-gather.2
  92.5 34.8 all-gather.4
  141.1 75.2 all-reduce.1
  219.0 43.8 reduce-scatter.1
where the time goes:
time: 317 us; the launch traced here: 316 us
  waiting for transfers between devices  155 us (49%)
  blocking collectives  79.3 us (25%)
  starting transfers between devices  30.5 us (10%)
  matrix products  19.2 us (6%)
  local copies, waits for them, and re-layouts  15 us (5%)
  between operations  14 us (4%)
  other arithmetic  3.41 us (1%)
    all_to_all x2, blocking collectives, exchange(): lax.all_to_all(rows.reshape(experts, CAP, width), 'expert', split_axis=0,...  79.3 us
    psum x1, waiting for transfers between devices, on_device(): hidden_vec = lax.psum(proj_part, ('dp', 'test'))  66.4 us
    all_gather x2, waiting for transfers between devices, spread(): full = lax.all_gather(rows, ('dp', 'test'), axis=0, tiled=True)  31.3 us
    all_to_all x2, starting transfers between devices, exchange(): lax.all_to_all(rows.reshape(experts, CAP, width), 'expert', split_axis=0,...  30.3 us
    reduce_scatter x1, waiting for transfers between devices, on_device(): lax.psum_scatter(parts.reshape(groups * halves * slots, half), ('dp', 'te...  29.1 us
    all_to_all x2, waiting for transfers between devices, exchange(): lax.all_to_all(rows.reshape(experts, CAP, width), 'expert', split_axis=0,...  28.2 us
    dot_general x18, matrix products, dot(): lax.dot_general(a, b, (((ca,), (cb,)), ((), ())), preferred_element_type=...  19.2 us
  transfers between devices with their start and end apart: 6, of which 4 were waited for; matrix products, arithmetic and copies ran while one was open for 5% of the time, Pallas kernels for 0%

commit v1 on v0

--- a/solution.py
+++ b/solution.py
@@ -50,7 +50,10 @@
         return moved.reshape(slots, width)
 
     def spread(rows):
-        full = lax.all_gather(rows, ("dp", "test"), axis=0, tiled=True)
+        full = jnp.concatenate(
+            lax.all_to_all(jnp.stack([rows] * lax.axis_size(("dp", "test"))), ("dp", "test"), 0, 0),
+            axis=0,
+        )
         full = full.reshape(groups, halves, slots, half)
         return [full[:, h].reshape(groups * slots, half) for h in range(halves)]
 

time: 317 us -> 372 us (1.17)
  waiting for transfers between devices: 155 us -> 244 us
  blocking collectives: 79.3 us -> 0 us
  starting transfers between devices: 30.5 us -> 71.5 us
    all_to_all x2 -> x0, blocking collectives: 79.3 us -> none  [exchange(): lax.all_to_all(rows.reshape(experts, CAP, width), 'expert', split_axis=0,...]
    all_to_all x0 -> x2, waiting for transfers between devices: none -> 76.6 us  [spread(): lax.all_to_all(jnp.stack([rows] * lax.axis_size(('dp', 'test'))), ('dp',...]
    all_to_all x2 -> x4, waiting for transfers between devices: 28.2 us -> 80.2 us  [exchange(): lax.all_to_all(rows.reshape(experts, CAP, width), 'expert', split_axis=0,...]
    all_gather x2 -> x0, waiting for transfers between devices: 31.3 us -> none  [spread(): full = lax.all_gather(rows, ('dp', 'test'), axis=0, tiled=True)]
    all_to_all x2 -> x4, starting transfers between devices: 30.3 us -> 56.5 us  [exchange(): lax.all_to_all(rows.reshape(experts, CAP, width), 'expert', split_axis=0,...]
    all_to_all x0 -> x2, starting transfers between devices: none -> 15 us  [spread(): lax.all_to_all(jnp.stack([rows] * lax.axis_size(('dp', 'test'))), ('dp',...]
    psum x1, waiting for transfers between devices: 66.4 us -> 57.5 us  [on_device(): hidden_vec = lax.psum(proj_part, ('dp', 'test'))]
    another operation x0 -> x4, local copies, waits for them, and re-layouts: none -> 4.56 us  [spread(): jnp.stack([rows] * lax.axis_size(('dp', 'test')))]
  transfers between devices with their start and end apart: 6 -> 8, of which waited for: 4 -> 7; matrix products, arithmetic and copies ran while one was open for 5% -> 5% of each run, Pallas kernels for 0% -> 0%
where the time goes in v1:
time: 372 us; the launch traced here: 371 us
  waiting for transfers between devices  244 us (66%)
  starting transfers between devices  71.5 us (19%)
  matrix products  19.8 us (5%)
  local copies, waits for them, and re-layouts  18.1 us (5%)
  between operations  14.3 us (4%)
    all_to_all x4, waiting for transfers between devices, exchange(): lax.all_to_all(rows.reshape(experts, CAP, width), 'expert', split_axis=0,...  80.2 us
    all_to_all x2, waiting for transfers between devices, spread(): lax.all_to_all(jnp.stack([rows] * lax.axis_size(('dp', 'test'))), ('dp',...  76.6 us
    psum x1, waiting for transfers between devices, on_device(): hidden_vec = lax.psum(proj_part, ('dp', 'test'))  57.5 us
    all_to_all x4, starting transfers between devices, exchange(): lax.all_to_all(rows.reshape(experts, CAP, width), 'expert', split_axis=0,...  56.5 us
    reduce_scatter x1, waiting for transfers between devices, on_device(): lax.psum_scatter(parts.reshape(groups * halves * slots, half), ('dp', 'te...  29.3 us
    dot_general x18, matrix products, dot(): lax.dot_general(a, b, (((ca,), (cb,)), ((), ())), preferred_element_type=...  19.8 us
    all_to_all x2, starting transfers between devices, spread(): lax.all_to_all(jnp.stack([rows] * lax.axis_size(('dp', 'test'))), ('dp',...  15 us
  transfers between devices with their start and end apart: 8, of which 7 were waited for; matrix products, arithmetic and copies ran while one was open for 5% of the time, Pallas kernels for 0%

profile of v1, /device:TPU:31, one launch (start us, length us, event | category | flops | bytes accessed | tf_op | source)
XLA Modules:
  0.0 370.7 jit_solution(9035887714529227340)
XLA Ops:
  7.2 0.8 add_select_fusion
  9.1 1.2 convolution_convert_fusion
  10.4 1.0 reshape.51
  11.3 18.2 %all-to-all-start.2 = ((bf16[64,2,1792]{2,1,0:T(2,128)(2,1)}), bf16[64,2,1792]{2,1,0:T(2,128)(2,1)S(1)}, u32[]{:S(2)}, u32[]{:S(2)}) async-start(bf16[64,2,1792]{2,1,0:T(2,128)(2,1)} %reshape.51), calls=%async_computation.2 | async-start | bytes 917504 | tf_op jit(solution)/shard_map/all_to_all | solution.py:47
  29.9 1.0 reshape.50
  30.8 26.0 %all-to-all-done.2 = bf16[64,2,1792]{2,1,0:T(2,128)(2,1)S(1)} async-done(((bf16[64,2,1792]{2,1,0:T(2,128)(2,1)}), bf16[64,2,1792]{2,1,0:T(2,128)(2,1)S(1)}, u32[]{:S(2)}, u32[]{:S(2)}) %all-to-all-start.2) | async-done | bytes 458784 | tf_op jit(solution)/shard_map/all_to_all | solution.py:47
  56.8 7.9 %all-to-all-start = ((bf16[64,2,1792]{2,1,0:T(2,128)(2,1)}), bf16[64,2,1792]{2,1,0:T(2,128)(2,1)S(1)}, u32[]{:S(2)}, u32[]{:S(2)}) async-start(bf16[64,2,1792]{2,1,0:T(2,128)(2,1)} %reshape.50), calls=%async_computation | async-start | bytes 917504 | tf_op jit(solution)/shard_map/all_to_all | solution.py:47
  64.9 26.0 %all-to-all-done = bf16[64,2,1792]{2,1,0:T(2,128)(2,1)S(1)} async-done(((bf16[64,2,1792]{2,1,0:T(2,128)(2,1)}), bf16[64,2,1792]{2,1,0:T(2,128)(2,1)S(1)}, u32[]{:S(2)}, u32[]{:S(2)}) %all-to-all-start) | async-done | bytes 458784 | tf_op jit(solution)/shard_map/all_to_all | solution.py:47
  90.9 2.0 stack.10
  93.0 7.9 %all-to-all-start.3 = ((bf16[8,128,1792]{2,1,0:T(8,128)(2,1)}), bf16[8,128,1792]{2,1,0:T(8,128)(2,1)}, u32[]{:S(2)}, u32[]{:S(2)}) async-start(bf16[8,128,1792]{2,1,0:T(8,128)(2,1)} %stack.10), calls=%async_computation.3 | async-start | bytes 7340032 | tf_op jit(solution)/shard_map/all_to_all | solution.py:54
  101.1 41.3 %all-to-all-done.3 = bf16[8,128,1792]{2,1,0:T(8,128)(2,1)} async-done(((bf16[8,128,1792]{2,1,0:T(8,128)(2,1)}), bf16[8,128,1792]{2,1,0:T(8,128)(2,1)}, u32[]{:S(2)}, u32[]{:S(2)}) %all-to-all-start.3) | async-done | bytes 3670048 | tf_op jit(solution)/shard_map/all_to_all | solution.py:54
  142.4 2.2 stack.9
  144.6 7.1 %all-to-all-start.1 = ((bf16[8,128,1792]{2,1,0:T(8,128)(2,1)}), bf16[8,128,1792]{2,1,0:T(8,128)(2,1)}, u32[]{:S(2)}, u32[]{:S(2)}) async-start(bf16[8,128,1792]{2,1,0:T(8,128)(2,1)} %stack.9), calls=%async_computation.1 | async-start | bytes 7340032 | tf_op jit(solution)/shard_map/all_to_all | solution.py:54
  151.7 2.4 fusion.42
  156.5 1.3 convolution_add_fusion
  157.9 35.3 %all-to-all-done.1 = bf16[8,128,1792]{2,1,0:T(8,128)(2,1)} async-done(((bf16[8,128,1792]{2,1,0:T(8,128)(2,1)}), bf16[8,128,1792]{2,1,0:T(8,128)(2,1)}, u32[]{:S(2)}, u32[]{:S(2)}) %all-to-all-start.1) | async-done | bytes 3670048 | tf_op jit(solution)/shard_map/all_to_all | solution.py:54
  193.1 2.4 fusion.41
  197.8 2.4 fusion.4
  200.3 2.5 fusion.7
  202.8 0.9 fusion.30
  203.7 3.0 add_convert_fusion
  207.9 2.1 pad_maximum_fusion
  210.0 1.0 copy-done.7
  211.3 1.3 convolution_add_fusion.3
  212.6 57.5 %all-reduce.2.cloned.1.call-done = f32[512,64]{0,1:T(8,128)} async-done(((f32[512,64]{0,1:T(8,128)}), f32[512,64]{0,1:T(8,128)}) %all-reduce.2.cloned.1.call-update) | async-done | bytes 131088 | tf_op jit(solution)/shard_map/psum | solution.py:93
  271.2 1.1 convolution_convert_fusion.3
  272.3 15.3 %all-to-all-start.5 = ((bf16[64,2,128]{2,1,0:T(2,128)(2,1)}), bf16[64,2,128]{2,1,0:T(2,128)(2,1)S(1)}, u32[]{:S(2)}, u32[]{:S(2)}) async-start(bf16[64,2,128]{2,1,0:T(2,128)(2,1)} %bitcast.20), calls=%async_computation.6 | async-start | bytes 65536 | tf_op jit(solution)/shard_map/all_to_all | solution.py:47
  287.7 29.3 %reduce-scatter.2.cloned.1.call-done = bf16[128,1792]{1,0:T(8,128)(2,1)} async-done(((bf16[1024,1792]{1,0:T(8,128)(2,1)}), bf16[128,1792]{1,0:T(8,128)(2,1)}) %reduce-scatter.2.cloned.1.call-update) | async-done | bytes 458768 | tf_op jit(solution)/shard_map/reduce_scatter | solution.py:85
  316.9 2.0 reshape.53
  318.9 15.0 %all-to-all-start.4 = ((bf16[64,2,1792]{2,1,0:T(2,128)(2,1)}), bf16[64,2,1792]{2,1,0:T(2,128)(2,1)S(1)}, u32[]{:S(2)}, u32[]{:S(2)}) async-start(bf16[64,2,1792]{2,1,0:T(2,128)(2,1)} %reshape.53), calls=%async_computation.5 | async-start | bytes 917504 | tf_op jit(solution)/shard_map/all_to_all | solution.py:47
  334.6 28.2 %all-to-all-done.4 = bf16[64,2,1792]{2,1,0:T(2,128)(2,1)S(1)} async-done(((bf16[64,2,1792]{2,1,0:T(2,128)(2,1)}), bf16[64,2,1792]{2,1,0:T(2,128)(2,1)S(1)}, u32[]{:S(2)}, u32[]{:S(2)}) %all-to-all-start.4) | async-done | bytes 458784 | tf_op jit(solution)/shard_map/all_to_all | solution.py:47
  362.9 0.9 convolution_convert_fusion.2
  (45 shorter events, 10.0 us)
Async XLA Ops:
  7.2 264.0 %copy-start = (bf16[1,128,4096]{2,1,0:T(8,128)(2,1)S(1)}, bf16[1,128,4096]{2,1,0:T(8,128)(2,1)}, u32[]{:S(2)}) copy-start(bf16[1,128,4096]{2,1,0:T(8,128)(2,1)} %param.21) | copy-start | bytes 3145732
  7.2 22.4 %copy-start.10 = (bf16[64,1792]{1,0:T(8,128)(2,1)S(1)}, bf16[64,1792]{1,0:T(8,128)(2,1)}, u32[]{:S(2)}) copy-start(bf16[64,1792]{1,0:T(8,128)(2,1)} %param.12) | copy-start | bytes 688132
  11.3 45.5 %all-to-all-start.2 = ((bf16[64,2,1792]{2,1,0:T(2,128)(2,1)}), bf16[64,2,1792]{2,1,0:T(2,128)(2,1)S(1)}, u32[]{:S(2)}, u32[]{:S(2)}) async-start(bf16[64,2,1792]{2,1,0:T(2,128)(2,1)} %reshape.51), calls=%async_computation.2 | async-start | bytes 917504 | tf_op jit(solution)/shard_map/all_to_all | solution.py:47
  56.8 34.1 %all-to-all-start = ((bf16[64,2,1792]{2,1,0:T(2,128)(2,1)}), bf16[64,2,1792]{2,1,0:T(2,128)(2,1)S(1)}, u32[]{:S(2)}, u32[]{:S(2)}) async-start(bf16[64,2,1792]{2,1,0:T(2,128)(2,1)} %reshape.50), calls=%async_computation | async-start | bytes 917504 | tf_op jit(solution)/shard_map/all_to_all | solution.py:47
  93.0 49.4 %all-to-all-start.3 = ((bf16[8,128,1792]{2,1,0:T(8,128)(2,1)}), bf16[8,128,1792]{2,1,0:T(8,128)(2,1)}, u32[]{:S(2)}, u32[]{:S(2)}) async-start(bf16[8,128,1792]{2,1,0:T(8,128)(2,1)} %stack.10), calls=%async_computation.3 | async-start | bytes 7340032 | tf_op jit(solution)/shard_map/all_to_all | solution.py:54
  144.6 48.5 %all-to-all-start.1 = ((bf16[8,128,1792]{2,1,0:T(8,128)(2,1)}), bf16[8,128,1792]{2,1,0:T(8,128)(2,1)}, u32[]{:S(2)}, u32[]{:S(2)}) async-start(bf16[8,128,1792]{2,1,0:T(8,128)(2,1)} %stack.9), calls=%async_computation.1 | async-start | bytes 7340032 | tf_op jit(solution)/shard_map/all_to_all | solution.py:54
  151.6 118.5 %all-reduce.2.cloned.1.call-start = ((), (), s32[]{:S(2)}) async-start(), calls=%async_computation.8 | async-start | bytes 262144 | tf_op jit(solution)/shard_map/psum | solution.py:93
  151.7 2.4 copy-start.2
  154.0 1.2 copy-start.4
  193.1 2.4 copy-start.9
  195.5 1.8 copy-start.6
  195.5 1.1 copy-start.8
  196.7 1.2 copy-start.3
  200.3 2.5 copy-start.11
  203.7 113.2 %reduce-scatter.2.cloned.1.call-start = ((), (), s32[]{:S(2)}) async-start(), calls=%async_computation.7 | async-start | bytes 4128768 | tf_op jit(solution)/shard_map/reduce_scatter | solution.py:85
  203.7 3.3 copy-start.1
  203.7 3.5 copy-start.5
  210.0 1.0 copy-start.7
  272.3 46.6 %all-to-all-start.5 = ((bf16[64,2,128]{2,1,0:T(2,128)(2,1)}), bf16[64,2,128]{2,1,0:T(2,128)(2,1)S(1)}, u32[]{:S(2)}, u32[]{:S(2)}) async-start(bf16[64,2,128]{2,1,0:T(2,128)(2,1)} %bitcast.20), calls=%async_computation.6 | async-start | bytes 65536 | tf_op jit(solution)/shard_map/all_to_all | solution.py:47
  318.9 43.9 %all-to-all-start.4 = ((bf16[64,2,1792]{2,1,0:T(2,128)(2,1)}), bf16[64,2,1792]{2,1,0:T(2,128)(2,1)S(1)}, u32[]{:S(2)}, u32[]{:S(2)}) async-start(bf16[64,2,1792]{2,1,0:T(2,128)(2,1)} %reshape.53), calls=%async_computation.5 | async-start | bytes 917504 | tf_op jit(solution)/shard_map/all_to_all | solution.py:47
Sparse Core Ops, SparseCore 0:
  203.8 66.3 all-reduce.1
  273.0 43.8 reduce-scatter.1
